TPU v7x, 32 devices: a whole 2x2x4 slice. The times are simulated.
32 devices in a mesh: seq: 16 (over z, x, core), head: 2 (over y).
Axes of the slice: x: 2, y: 2, z: 4, core: 2. Of those that a mesh axis runs over, the one named last changes fastest.
Arguments:
- queries: bfloat16 [2048, 2048], P('seq', 'head'), may hold values from -5 to 5
- keys: bfloat16 [2048, 2048], P('seq', 'head'), may hold values from -5 to 5
- values: bfloat16 [2048, 2048], P('seq', 'head'), may hold values from -6 to 6
- grad_out: bfloat16 [2048, 2048], P('seq', 'head'), may hold values from -6 to 6
- doc_ids: int32 [2048], P(('seq', 'head')), may hold values from 0 to 31, never falling along the last dimension, each value on 1 to 512 neighbouring positions
- loss_mask: int32 [2048], P(('seq', 'head')), may hold values 0 or 1
Outputs:
- attended: bfloat16 [2048, 2048], P('seq', 'head')
- query_grad: bfloat16 [2048, 2048], P('seq', 'head')
- key_grad: bfloat16 [2048, 2048], P('seq', 'head')
- value_grad: bfloat16 [2048, 2048], P('seq', 'head')
Inputs may be any that keep to these rules, and one draw needn't show every extreme that they name: `doc_ids`: documents are runs of consecutive tokens numbered 0, 1, 2, ... in order; each has 1 to 512 tokens.
All inputs are finite; a program needn't handle non-finite values. No bound on the sum of `loss_mask` on one device may be relied on, other than what follows from the above.
Results may differ from a plain program's by a relative error of at most 0.033.
Values may be sent and summed in bfloat16 or wider, within the bound.
No kernel may reach another device: no remote copies, remote signals or barrier semaphores. Data moves between devices by JAX's collectives and lax.ppermute only.
A program may use at most 64 MiB of HBM per device.

v0:
```python
from functools import reduce
import math

import jax
import jax.numpy as jnp
from jax import lax
from jax.sharding import PartitionSpec as P

HEAD_DIM = 128
REACH = 4
WINDOW = 512


masked_value = -1e30
big_index = 2**30


def shifted(block, axis, distance):
    devices = range(lax.axis_size(axis))
    route = [(i - distance, i) for i in devices if i - distance in devices]
    return lax.ppermute(block, axis, route)


def for_sending(value):

    def short(part):
        return part.astype(jnp.bfloat16) if part.dtype == jnp.float32 else part

    return jax.tree.map(short, value)


def allowed_for(q_pos, q_start, k_pos):
    later = k_pos[None, :] <= q_pos[:, None]
    inside = k_pos[None, :] > q_pos[:, None] - WINDOW
    same_doc = k_pos[None, :] >= q_start[:, None]
    return later & inside & same_doc


def by_head(rows):
    return rows.reshape(rows.shape[0], -1, HEAD_DIM)


def tile_scores(q_rows, k_rows, allowed):
    score = jnp.einsum(
        "qhd,khd->hqk", by_head(q_rows), by_head(k_rows), preferred_element_type=jnp.float32
    )
    return jnp.where(allowed[None], score * (1.0 / math.sqrt(HEAD_DIM)), masked_value)


def tile_mix(prob, v_rows):
    return jnp.einsum(
        "hqk,khd->qhd",
        prob.astype(jnp.bfloat16),
        by_head(v_rows),
        preferred_element_type=jnp.float32,
    )


def grad_of_scores(g_rows, v_rows, prob, row_delta):
    prob_grad = jnp.einsum(
        "qhd,khd->hqk", by_head(g_rows), by_head(v_rows), preferred_element_type=jnp.float32
    )
    return (prob * (prob_grad - row_delta[..., None]) * (1.0 / math.sqrt(HEAD_DIM))).astype(
        jnp.bfloat16
    )


def key_terms_of(q_rows, g_rows, k_rows, prob, score_grad):
    key_part = jnp.einsum(
        "hqk,qhd->khd", score_grad, by_head(q_rows), preferred_element_type=jnp.float32
    )
    value_part = jnp.einsum(
        "hqk,qhd->khd",
        prob.astype(jnp.bfloat16),
        by_head(g_rows),
        preferred_element_type=jnp.float32,
    )
    return (key_part.reshape(k_rows.shape), value_part.reshape(k_rows.shape))


def tile_back(q_rows, g_rows, k_rows, v_rows, prob, row_delta):
    score_grad = grad_of_scores(g_rows, v_rows, prob, row_delta)
    result = jnp.einsum(
        "hqk,khd->qhd", score_grad, by_head(k_rows), preferred_element_type=jnp.float32
    )
    key_part, value_part = key_terms_of(q_rows, g_rows, k_rows, prob, score_grad)
    return (result.reshape(q_rows.shape), key_part, value_part)


def body(queries, keys, values, grad_out, doc_ids, loss_mask):
    block_rows, width = queries.shape
    seq_index = lax.axis_index("seq")
    doc_rows, mask_rows = (
        lax.all_gather(doc_ids, "head", axis=0, tiled=True),
        lax.all_gather(loss_mask, "head", axis=0, tiled=True),
    )
    positions = seq_index * block_rows + jnp.arange(block_rows, dtype=jnp.int32)
    catalog = jnp.arange(2 * lax.axis_size("seq"), dtype=jnp.int32)
    member = doc_rows[:, None] == catalog[None, :]
    local_counts = jnp.sum(jnp.where(member, mask_rows[:, None].astype(jnp.float32), 0.0), axis=0)
    local_first = jnp.min(jnp.where(member, positions[:, None], big_index), axis=0)
    counts = lax.psum(local_counts, "seq")
    firsts = lax.pmin(local_first, "seq")
    doc_start = jnp.sum(jnp.where(member, firsts[None, :], 0), axis=1)
    doc_count = jnp.sum(jnp.where(member, counts[None, :], 0.0), axis=1)
    weight = (
        mask_rows.astype(jnp.float32) * block_rows / jnp.maximum(doc_count, float(block_rows // 8))
    )
    remote = []
    carried = (keys, values)
    for distance in range(1, REACH + 1):
        carried = shifted((carried[0], carried[1]), "seq", 1)
        remote.append(carried)
    key_blocks = [(keys, values)] + remote
    masks = [
        allowed_for(positions, doc_start, positions - distance * block_rows)
        for distance in range(REACH + 1)
    ]
    score_list = [
        tile_scores(queries, key_blocks[distance][0], masks[distance])
        for distance in range(REACH + 1)
    ]
    row_max = reduce(jnp.maximum, [jnp.max(score, axis=2) for score in score_list])
    row_sum = sum((jnp.sum(jnp.exp(score - row_max[..., None]), axis=2) for score in score_list))
    log_total = row_max + jnp.log(row_sum)
    prob_list = [jnp.exp(score - log_total[..., None]) for score in score_list]
    mixed_out = sum(
        (tile_mix(prob_list[distance], key_blocks[distance][1]) for distance in range(REACH + 1))
    )
    attended = mixed_out.astype(jnp.bfloat16).reshape(block_rows, width)
    grad_rows = (weight[:, None] * grad_out.astype(jnp.float32)).astype(jnp.bfloat16)
    row_delta = jnp.sum(
        by_head(grad_rows).astype(jnp.float32) * by_head(attended).astype(jnp.float32), axis=2
    ).T
    terms = [
        tile_back(
            queries,
            grad_rows,
            key_blocks[distance][0],
            key_blocks[distance][1],
            prob_list[distance],
            row_delta,
        )
        for distance in range(REACH + 1)
    ]
    query_total = sum((term[0] for term in terms))
    carried = (terms[REACH][1], terms[REACH][2])
    for distance in range(REACH - 1, -1, -1):
        carried = shifted((for_sending(carried[0]), for_sending(carried[1])), "seq", -1)
        carried = (carried[0] + terms[distance][1], carried[1] + terms[distance][2])
    return (
        attended,
        query_total.astype(jnp.bfloat16),
        carried[0].astype(jnp.bfloat16),
        carried[1].astype(jnp.bfloat16),
    )


def solution(mesh):
    placed = (
        P("seq", "head"),
        P("seq", "head"),
        P("seq", "head"),
        P("seq", "head"),
        P(("seq", "head")),
        P(("seq", "head")),
    )
    return jax.shard_map(
        body,
        mesh=mesh,
        in_specs=placed,
        out_specs=(P("seq", "head"), P("seq", "head"), P("seq", "head"), P("seq", "head")),
        check_vma=False,
    )
```

profile of v0, /device:TPU:7, one launch (start us, length us, event | category | flops | bytes accessed | tf_op | source)
XLA Modules:
  0.0 141.8 jit_solution(1139178747998458815)
XLA Ops:
  1.8 3.7 %collective-permute-start = (bf16[128,1024]{0,1:T(8,128)(2,1)S(1)}, bf16[128,1024]{0,1:T(8,128)(2,1)S(1)}, u32[]{:S(2)}, u32[]{:S(2)}) collective-permute-start(bf16[128,1024]{0,1:T(8,128)(2,1)S(1)} %copy.258), channel_id=1, source_target_pairs={{0,2},{2,4},{4,6},{6,8},{8,10},{10,12},{12,14},{14,16},{16,18},{18... | collective-permute-start | bytes 786440 | tf_op jit(solution)/shard_map/ppermute | solution.py:21
  5.6 1.9 %collective-permute-start.4 = (bf16[128,1024]{1,0:T(8,128)(2,1)S(1)}, bf16[128,1024]{1,0:T(8,128)(2,1)S(1)}, u32[]{:S(2)}, u32[]{:S(2)}) collective-permute-start(bf16[128,1024]{1,0:T(8,128)(2,1)S(1)} %copy-done.19), channel_id=1, source_target_pairs={{0,2},{2,4},{4,6},{6,8},{8,10},{10,12},{12,14},{14,16},{16,18},{18... | collective-permute-start | bytes 786440 | tf_op jit(solution)/shard_map/ppermute | solution.py:21
  11.1 3.1 %all-reduce.2 = (s32[128]{0:T(128)S(1)}, s32[128]{0:T(128)S(1)}) all-reduce(s32[128]{0:T(128)S(1)} %dynamic-update-slice, s32[128]{0:T(128)S(1)} %dynamic-update-slice.1), channel_id=1, replica_groups=mesh['seq'=16,'head'=2] {'head'}, use_global_device_ids=true, to_apply=%add | all-reduce | flops 256 | bytes 2048
  14.4 9.8 %pmin.7 = s32[32]{0:T(128)S(1)} all-reduce(s32[32]{0:T(128)S(1)} %select_reduce_fusion.3), channel_id=1, replica_groups=mesh['seq'=16,'head'=2] {'seq'}, use_global_device_ids=true, to_apply=%region_1.2 | all-reduce | flops 32 | bytes 256 | tf_op jit(solution)/shard_map/pmin | solution.py:103
  24.8 27.8 %psum.7 = f32[32]{0:T(128)S(1)} all-reduce(f32[32]{0:T(128)S(1)} %select_reduce_fusion.1), channel_id=1, replica_groups=mesh['seq'=16,'head'=2] {'seq'}, use_global_device_ids=true, to_apply=%region_14.15 | all-reduce | flops 32 | bytes 256 | tf_op jit(solution)/shard_map/psum | solution.py:102
  52.9 1.9 %collective-permute-start.1 = (bf16[128,1024]{0,1:T(8,128)(2,1)S(1)}, bf16[128,1024]{0,1:T(8,128)(2,1)S(1)}, u32[]{:S(2)}, u32[]{:S(2)}) collective-permute-start(bf16[128,1024]{0,1:T(8,128)(2,1)S(1)} %collective-permute-done), channel_id=1, source_target_pairs={{0,2},{2,4},{4,6},{6,8},{8,10},{10,12},{12,14},{14,16},{16,18},{18... | collective-permute-start | bytes 786440 | tf_op jit(solution)/shard_map/ppermute | solution.py:21
  54.9 1.9 %collective-permute-start.5 = (bf16[128,1024]{1,0:T(8,128)(2,1)S(1)}, bf16[128,1024]{1,0:T(8,128)(2,1)S(1)}, u32[]{:S(2)}, u32[]{:S(2)}) collective-permute-start(bf16[128,1024]{1,0:T(8,128)(2,1)S(1)} %collective-permute-done.4), channel_id=1, source_target_pairs={{0,2},{2,4},{4,6},{6,8},{8,10},{10,12},{12,14},{14,16},{16,18},{18... | collective-permute-start | bytes 786440 | tf_op jit(solution)/shard_map/ppermute | solution.py:21
  58.1 5.3 %collective-permute-start.2 = (bf16[128,1024]{0,1:T(8,128)(2,1)S(1)}, bf16[128,1024]{0,1:T(8,128)(2,1)}, u32[]{:S(2)}, u32[]{:S(2)}) collective-permute-start(bf16[128,1024]{0,1:T(8,128)(2,1)S(1)} %collective-permute-done.1), channel_id=1, source_target_pairs={{0,2},{2,4},{4,6},{6,8},{8,10},{10,12},{12,14},{14,16},{16,18},{18... | collective-permute-start | bytes 786440 | tf_op jit(solution)/shard_map/ppermute | solution.py:21
  63.7 2.5 %collective-permute-start.6 = (bf16[128,1024]{1,0:T(8,128)(2,1)S(1)}, bf16[128,1024]{1,0:T(8,128)(2,1)}, u32[]{:S(2)}, u32[]{:S(2)}) collective-permute-start(bf16[128,1024]{1,0:T(8,128)(2,1)S(1)} %collective-permute-done.5), channel_id=1, source_target_pairs={{0,2},{2,4},{4,6},{6,8},{8,10},{10,12},{12,14},{14,16},{16,18},{18... | collective-permute-start | bytes 786440 | tf_op jit(solution)/shard_map/ppermute | solution.py:21
  67.0 5.1 %collective-permute-start.3 = (bf16[128,1024]{0,1:T(8,128)(2,1)}, bf16[128,1024]{0,1:T(8,128)(2,1)S(1)}, u32[]{:S(2)}, u32[]{:S(2)}) collective-permute-start(bf16[128,1024]{0,1:T(8,128)(2,1)} %collective-permute-done.2), channel_id=1, source_target_pairs={{0,2},{2,4},{4,6},{6,8},{8,10},{10,12},{12,14},{14,16},{16,18},{18... | collective-permute-start | bytes 786440 | tf_op jit(solution)/shard_map/ppermute | solution.py:21
  73.3 1.8 %copy.166 = bf16[128,1024]{0,1:T(8,128)(2,1)} copy(bf16[128,1024]{1,0:T(8,128)(2,1)} %collective-permute-done.6) | data formatting | bytes 524288 | tf_op jit(solution)/shard_map/ppermute | solution.py:21
  75.1 1.9 %collective-permute-start.7 = (bf16[128,1024]{1,0:T(8,128)(2,1)}, bf16[128,1024]{1,0:T(8,128)(2,1)}, u32[]{:S(2)}, u32[]{:S(2)}) collective-permute-start(bf16[128,1024]{1,0:T(8,128)(2,1)} %collective-permute-done.6), channel_id=1, source_target_pairs={{0,2},{2,4},{4,6},{6,8},{8,10},{10,12},{12,14},{14,16},{16,18},{18... | collective-permute-start | bytes 786440 | tf_op jit(solution)/shard_map/ppermute | solution.py:21
  84.4 1.8 %copy.168 = bf16[128,1024]{0,1:T(8,128)(2,1)} copy(bf16[128,1024]{1,0:T(8,128)(2,1)} %collective-permute-done.7) | data formatting | bytes 524288 | tf_op jit(solution)/shard_map/ppermute | solution.py:21
  86.2 2.1 %multiply_reduce_fusion = (f32[128,8]{0,1:T(8,128)S(1)}, bf16[8,128,128]{1,2,0:T(8,128)(2,1)}) fusion(bf16[128,1024]{0,1:T(8,128)(2,1)S(1)} %copy.170, f32[8,128,128]{1,2,0:T(8,128)} %convolution_add_fusion.5, bf16[128,8,128]{0,2,1:T(8,128)(2,1)} %bitcast.137, f32[8,128,128]{1,2,0:T(8,128)S(1)} %get-tuple-element.29, f32[8,128]{1,0:T(8,128)S(1)} %log_add_fusion), kind=kOutput, calls=%fused_computation.50 | convolution fusion | flops 34601984 | bytes 1843200 | tf_op jit(solution)/shard_map/hqk,khd->qhd/dot_general | solution.py:51
  100.4 3.4 %collective-permute-start.8 = (bf16[128,1024]{1,0:T(8,128)(2,1)S(1)}, bf16[128,1024]{1,0:T(8,128)(2,1)S(1)}, u32[]{:S(2)}, u32[]{:S(2)}) collective-permute-start(bf16[128,1024]{1,0:T(8,128)(2,1)S(1)} %copy.194), channel_id=1, source_target_pairs={{2,0},{4,2},{6,4},{8,6},{10,8},{12,10},{14,12},{16,14},{18,16},{20... | collective-permute-start | bytes 786440 | tf_op jit(solution)/shard_map/ppermute | solution.py:21
  104.3 3.6 %collective-permute-start.12 = (bf16[128,1024]{1,0:T(8,128)(2,1)S(1)}, bf16[128,1024]{1,0:T(8,128)(2,1)S(1)}, u32[]{:S(2)}, u32[]{:S(2)}) collective-permute-start(bf16[128,1024]{1,0:T(8,128)(2,1)S(1)} %copy.208), channel_id=1, source_target_pairs={{2,0},{4,2},{6,4},{8,6},{10,8},{12,10},{14,12},{16,14},{18,16},{20... | collective-permute-start | bytes 786440 | tf_op jit(solution)/shard_map/ppermute | solution.py:21
  109.6 3.2 %collective-permute-start.9 = (bf16[128,1024]{1,0:T(8,128)(2,1)S(1)}, bf16[128,1024]{1,0:T(8,128)(2,1)S(1)}, u32[]{:S(2)}, u32[]{:S(2)}) collective-permute-start(bf16[128,1024]{1,0:T(8,128)(2,1)S(1)} %add_convert_fusion.7), channel_id=1, source_target_pairs={{2,0},{4,2},{6,4},{8,6},{10,8},{12,10},{14,12},{16,14},{18,16},{20... | collective-permute-start | bytes 786440 | tf_op jit(solution)/shard_map/ppermute | solution.py:21
  112.9 2.5 %collective-permute-start.13 = (bf16[128,1024]{1,0:T(8,128)(2,1)S(1)}, bf16[128,1024]{1,0:T(8,128)(2,1)}, u32[]{:S(2)}, u32[]{:S(2)}) collective-permute-start(bf16[128,1024]{1,0:T(8,128)(2,1)S(1)} %add_convert_fusion.3), channel_id=1, source_target_pairs={{2,0},{4,2},{6,4},{8,6},{10,8},{12,10},{14,12},{16,14},{18,16},{20... | collective-permute-start | bytes 786440 | tf_op jit(solution)/shard_map/ppermute | solution.py:21
  118.4 2.2 %collective-permute-start.10 = (bf16[128,1024]{1,0:T(8,128)(2,1)S(1)}, bf16[128,1024]{1,0:T(8,128)(2,1)S(1)}, u32[]{:S(2)}, u32[]{:S(2)}) collective-permute-start(bf16[128,1024]{1,0:T(8,128)(2,1)S(1)} %add_convert_fusion.6), channel_id=1, source_target_pairs={{2,0},{4,2},{6,4},{8,6},{10,8},{12,10},{14,12},{16,14},{18,16},{20... | collective-permute-start | bytes 786440 | tf_op jit(solution)/shard_map/ppermute | solution.py:21
  122.6 1.9 %collective-permute-start.14 = (bf16[128,1024]{1,0:T(8,128)(2,1)S(1)}, bf16[128,1024]{1,0:T(8,128)(2,1)}, u32[]{:S(2)}, u32[]{:S(2)}) collective-permute-start(bf16[128,1024]{1,0:T(8,128)(2,1)S(1)} %add_convert_fusion.2), channel_id=1, source_target_pairs={{2,0},{4,2},{6,4},{8,6},{10,8},{12,10},{14,12},{16,14},{18,16},{20... | collective-permute-start | bytes 786440 | tf_op jit(solution)/shard_map/ppermute | solution.py:21
  127.2 2.2 %collective-permute-start.11 = (bf16[128,1024]{1,0:T(8,128)(2,1)S(1)}, bf16[128,1024]{1,0:T(8,128)(2,1)S(1)}, u32[]{:S(2)}, u32[]{:S(2)}) collective-permute-start(bf16[128,1024]{1,0:T(8,128)(2,1)S(1)} %add_convert_fusion.5), channel_id=1, source_target_pairs={{2,0},{4,2},{6,4},{8,6},{10,8},{12,10},{14,12},{16,14},{18,16},{20... | collective-permute-start | bytes 786440 | tf_op jit(solution)/shard_map/ppermute | solution.py:21
  129.4 2.0 %collective-permute-done.14 = bf16[128,1024]{1,0:T(8,128)(2,1)} collective-permute-done((bf16[128,1024]{1,0:T(8,128)(2,1)S(1)}, bf16[128,1024]{1,0:T(8,128)(2,1)}, u32[]{:S(2)}, u32[]{:S(2)}) %collective-permute-start.14) | collective-permute-done | bytes 262176 | tf_op jit(solution)/shard_map/ppermute | solution.py:21
  132.4 2.1 %collective-permute-start.15 = (bf16[128,1024]{1,0:T(8,128)(2,1)S(1)}, bf16[128,1024]{1,0:T(8,128)(2,1)S(1)}, u32[]{:S(2)}, u32[]{:S(2)}) collective-permute-start(bf16[128,1024]{1,0:T(8,128)(2,1)S(1)} %add_convert_fusion.1), channel_id=1, source_target_pairs={{2,0},{4,2},{6,4},{8,6},{10,8},{12,10},{14,12},{16,14},{18,16},{20... | collective-permute-start | bytes 786440 | tf_op jit(solution)/shard_map/ppermute | solution.py:21
  138.5 2.6 %collective-permute-done.15 = bf16[128,1024]{1,0:T(8,128)(2,1)S(1)} collective-permute-done((bf16[128,1024]{1,0:T(8,128)(2,1)S(1)}, bf16[128,1024]{1,0:T(8,128)(2,1)S(1)}, u32[]{:S(2)}, u32[]{:S(2)}) %collective-permute-start.15) | collective-permute-done | bytes 262176 | tf_op jit(solution)/shard_map/ppermute | solution.py:21
  (155 shorter events, 43.2 us)
Async XLA Ops:
  0.6 23.9 %copy-start.30 = (bf16[128,1024]{1,0:T(8,128)(2,1)S(1)}, bf16[128,1024]{1,0:T(8,128)(2,1)}, u32[]{:S(2)}) copy-start(bf16[128,1024]{1,0:T(8,128)(2,1)} %param.6) | copy-start | bytes 786436
  1.8 50.8 %copy-start.13 = (bf16[128,1024]{0,1:T(8,128)(2,1)}, bf16[128,1024]{0,1:T(8,128)(2,1)S(1)}, u32[]{:S(2)}) copy-start(bf16[128,1024]{0,1:T(8,128)(2,1)S(1)} %copy.258) | copy-start | bytes 786436
  1.8 51.0 %collective-permute-start = (bf16[128,1024]{0,1:T(8,128)(2,1)S(1)}, bf16[128,1024]{0,1:T(8,128)(2,1)S(1)}, u32[]{:S(2)}, u32[]{:S(2)}) collective-permute-start(bf16[128,1024]{0,1:T(8,128)(2,1)S(1)} %copy.258), channel_id=1, source_target_pairs={{0,2},{2,4},{4,6},{6,8},{8,10},{10,12},{12,14},{14,16},{16,18},{18... | collective-permute-start | bytes 786440 | tf_op jit(solution)/shard_map/ppermute | solution.py:21
  5.6 49.3 %collective-permute-start.4 = (bf16[128,1024]{1,0:T(8,128)(2,1)S(1)}, bf16[128,1024]{1,0:T(8,128)(2,1)S(1)}, u32[]{:S(2)}, u32[]{:S(2)}) collective-permute-start(bf16[128,1024]{1,0:T(8,128)(2,1)S(1)} %copy-done.19), channel_id=1, source_target_pairs={{0,2},{2,4},{4,6},{6,8},{8,10},{10,12},{12,14},{14,16},{16,18},{18... | collective-permute-start | bytes 786440 | tf_op jit(solution)/shard_map/ppermute | solution.py:21
  52.6 10.8 %copy-start.29 = (bf16[128,1024]{1,0:T(8,128)(2,1)S(1)}, bf16[128,1024]{1,0:T(8,128)(2,1)}, u32[]{:S(2)}) copy-start(bf16[128,1024]{1,0:T(8,128)(2,1)} %param.9) | copy-start | bytes 786436
  52.9 13.3 %copy-start.25 = (bf16[128,1024]{0,1:T(8,128)(2,1)}, bf16[128,1024]{0,1:T(8,128)(2,1)S(1)}, u32[]{:S(2)}) copy-start(bf16[128,1024]{0,1:T(8,128)(2,1)S(1)} %collective-permute-done) | copy-start | bytes 786436
  52.9 5.2 %collective-permute-start.1 = (bf16[128,1024]{0,1:T(8,128)(2,1)S(1)}, bf16[128,1024]{0,1:T(8,128)(2,1)S(1)}, u32[]{:S(2)}, u32[]{:S(2)}) collective-permute-start(bf16[128,1024]{0,1:T(8,128)(2,1)S(1)} %collective-permute-done), channel_id=1, source_target_pairs={{0,2},{2,4},{4,6},{6,8},{8,10},{10,12},{12,14},{14,16},{16,18},{18... | collective-permute-start | bytes 786440 | tf_op jit(solution)/shard_map/ppermute | solution.py:21
  54.9 8.8 %collective-permute-start.5 = (bf16[128,1024]{1,0:T(8,128)(2,1)S(1)}, bf16[128,1024]{1,0:T(8,128)(2,1)S(1)}, u32[]{:S(2)}, u32[]{:S(2)}) collective-permute-start(bf16[128,1024]{1,0:T(8,128)(2,1)S(1)} %collective-permute-done.4), channel_id=1, source_target_pairs={{0,2},{2,4},{4,6},{6,8},{8,10},{10,12},{12,14},{14,16},{16,18},{18... | collective-permute-start | bytes 786440 | tf_op jit(solution)/shard_map/ppermute | solution.py:21
  58.1 14.0 %copy-start.27 = (bf16[128,1024]{0,1:T(8,128)(2,1)}, bf16[128,1024]{0,1:T(8,128)(2,1)S(1)}, u32[]{:S(2)}) copy-start(bf16[128,1024]{0,1:T(8,128)(2,1)S(1)} %collective-permute-done.1) | copy-start | bytes 786436
  58.1 8.9 %collective-permute-start.2 = (bf16[128,1024]{0,1:T(8,128)(2,1)S(1)}, bf16[128,1024]{0,1:T(8,128)(2,1)}, u32[]{:S(2)}, u32[]{:S(2)}) collective-permute-start(bf16[128,1024]{0,1:T(8,128)(2,1)S(1)} %collective-permute-done.1), channel_id=1, source_target_pairs={{0,2},{2,4},{4,6},{6,8},{8,10},{10,12},{12,14},{14,16},{16,18},{18... | collective-permute-start | bytes 786440 | tf_op jit(solution)/shard_map/ppermute | solution.py:21
  63.7 9.5 %collective-permute-start.6 = (bf16[128,1024]{1,0:T(8,128)(2,1)S(1)}, bf16[128,1024]{1,0:T(8,128)(2,1)}, u32[]{:S(2)}, u32[]{:S(2)}) collective-permute-start(bf16[128,1024]{1,0:T(8,128)(2,1)S(1)} %collective-permute-done.5), channel_id=1, source_target_pairs={{0,2},{2,4},{4,6},{6,8},{8,10},{10,12},{12,14},{14,16},{16,18},{18... | collective-permute-start | bytes 786440 | tf_op jit(solution)/shard_map/ppermute | solution.py:21
  67.0 11.2 %collective-permute-start.3 = (bf16[128,1024]{0,1:T(8,128)(2,1)}, bf16[128,1024]{0,1:T(8,128)(2,1)S(1)}, u32[]{:S(2)}, u32[]{:S(2)}) collective-permute-start(bf16[128,1024]{0,1:T(8,128)(2,1)} %collective-permute-done.2), channel_id=1, source_target_pairs={{0,2},{2,4},{4,6},{6,8},{8,10},{10,12},{12,14},{14,16},{16,18},{18... | collective-permute-start | bytes 786440 | tf_op jit(solution)/shard_map/ppermute | solution.py:21
  75.1 9.3 %collective-permute-start.7 = (bf16[128,1024]{1,0:T(8,128)(2,1)}, bf16[128,1024]{1,0:T(8,128)(2,1)}, u32[]{:S(2)}, u32[]{:S(2)}) collective-permute-start(bf16[128,1024]{1,0:T(8,128)(2,1)} %collective-permute-done.6), channel_id=1, source_target_pairs={{0,2},{2,4},{4,6},{6,8},{8,10},{10,12},{12,14},{14,16},{16,18},{18... | collective-permute-start | bytes 786440 | tf_op jit(solution)/shard_map/ppermute | solution.py:21
  88.5 7.9 %copy-start.5 = (bf16[8,128,128]{1,2,0:T(8,128)(2,1)}, bf16[8,128,128]{1,2,0:T(8,128)(2,1)S(1)}, u32[]{:S(2)}) copy-start(bf16[8,128,128]{1,2,0:T(8,128)(2,1)S(1)} %fusion.19) | copy-start | bytes 786436
  89.6 7.4 %copy-start.7 = (bf16[8,128,128]{1,2,0:T(8,128)(2,1)}, bf16[8,128,128]{1,2,0:T(8,128)(2,1)S(1)}, u32[]{:S(2)}) copy-start(bf16[8,128,128]{1,2,0:T(8,128)(2,1)S(1)} %fusion.15) | copy-start | bytes 786436
  100.4 9.1 %collective-permute-start.8 = (bf16[128,1024]{1,0:T(8,128)(2,1)S(1)}, bf16[128,1024]{1,0:T(8,128)(2,1)S(1)}, u32[]{:S(2)}, u32[]{:S(2)}) collective-permute-start(bf16[128,1024]{1,0:T(8,128)(2,1)S(1)} %copy.194), channel_id=1, source_target_pairs={{2,0},{4,2},{6,4},{8,6},{10,8},{12,10},{14,12},{16,14},{18,16},{20... | collective-permute-start | bytes 786440 | tf_op jit(solution)/shard_map/ppermute | solution.py:21
  104.3 8.6 %collective-permute-start.12 = (bf16[128,1024]{1,0:T(8,128)(2,1)S(1)}, bf16[128,1024]{1,0:T(8,128)(2,1)S(1)}, u32[]{:S(2)}, u32[]{:S(2)}) collective-permute-start(bf16[128,1024]{1,0:T(8,128)(2,1)S(1)} %copy.208), channel_id=1, source_target_pairs={{2,0},{4,2},{6,4},{8,6},{10,8},{12,10},{14,12},{16,14},{18,16},{20... | collective-permute-start | bytes 786440 | tf_op jit(solution)/shard_map/ppermute | solution.py:21
  109.6 8.7 %collective-permute-start.9 = (bf16[128,1024]{1,0:T(8,128)(2,1)S(1)}, bf16[128,1024]{1,0:T(8,128)(2,1)S(1)}, u32[]{:S(2)}, u32[]{:S(2)}) collective-permute-start(bf16[128,1024]{1,0:T(8,128)(2,1)S(1)} %add_convert_fusion.7), channel_id=1, source_target_pairs={{2,0},{4,2},{6,4},{8,6},{10,8},{12,10},{14,12},{16,14},{18,16},{20... | collective-permute-start | bytes 786440 | tf_op jit(solution)/shard_map/ppermute | solution.py:21
  112.9 8.7 %collective-permute-start.13 = (bf16[128,1024]{1,0:T(8,128)(2,1)S(1)}, bf16[128,1024]{1,0:T(8,128)(2,1)}, u32[]{:S(2)}, u32[]{:S(2)}) collective-permute-start(bf16[128,1024]{1,0:T(8,128)(2,1)S(1)} %add_convert_fusion.3), channel_id=1, source_target_pairs={{2,0},{4,2},{6,4},{8,6},{10,8},{12,10},{14,12},{16,14},{18,16},{20... | collective-permute-start | bytes 786440 | tf_op jit(solution)/shard_map/ppermute | solution.py:21
  118.4 8.7 %collective-permute-start.10 = (bf16[128,1024]{1,0:T(8,128)(2,1)S(1)}, bf16[128,1024]{1,0:T(8,128)(2,1)S(1)}, u32[]{:S(2)}, u32[]{:S(2)}) collective-permute-start(bf16[128,1024]{1,0:T(8,128)(2,1)S(1)} %add_convert_fusion.6), channel_id=1, source_target_pairs={{2,0},{4,2},{6,4},{8,6},{10,8},{12,10},{14,12},{16,14},{18,16},{20... | collective-permute-start | bytes 786440 | tf_op jit(solution)/shard_map/ppermute | solution.py:21
  122.6 8.7 %collective-permute-start.14 = (bf16[128,1024]{1,0:T(8,128)(2,1)S(1)}, bf16[128,1024]{1,0:T(8,128)(2,1)}, u32[]{:S(2)}, u32[]{:S(2)}) collective-permute-start(bf16[128,1024]{1,0:T(8,128)(2,1)S(1)} %add_convert_fusion.2), channel_id=1, source_target_pairs={{2,0},{4,2},{6,4},{8,6},{10,8},{12,10},{14,12},{16,14},{18,16},{20... | collective-permute-start | bytes 786440 | tf_op jit(solution)/shard_map/ppermute | solution.py:21
  127.2 7.3 %copy-start.6 = (bf16[8,128,128]{1,2,0:T(8,128)(2,1)S(1)}, bf16[8,128,128]{1,2,0:T(8,128)(2,1)}, u32[]{:S(2)}) copy-start(bf16[8,128,128]{1,2,0:T(8,128)(2,1)} %copy-done.5) | copy-start | bytes 786436
  127.2 10.5 %collective-permute-start.11 = (bf16[128,1024]{1,0:T(8,128)(2,1)S(1)}, bf16[128,1024]{1,0:T(8,128)(2,1)S(1)}, u32[]{:S(2)}, u32[]{:S(2)}) collective-permute-start(bf16[128,1024]{1,0:T(8,128)(2,1)S(1)} %add_convert_fusion.5), channel_id=1, source_target_pairs={{2,0},{4,2},{6,4},{8,6},{10,8},{12,10},{14,12},{16,14},{18,16},{20... | collective-permute-start | bytes 786440 | tf_op jit(solution)/shard_map/ppermute | solution.py:21
  132.4 8.7 %collective-permute-start.15 = (bf16[128,1024]{1,0:T(8,128)(2,1)S(1)}, bf16[128,1024]{1,0:T(8,128)(2,1)S(1)}, u32[]{:S(2)}, u32[]{:S(2)}) collective-permute-start(bf16[128,1024]{1,0:T(8,128)(2,1)S(1)} %add_convert_fusion.1), channel_id=1, source_target_pairs={{2,0},{4,2},{6,4},{8,6},{10,8},{12,10},{14,12},{16,14},{18,16},{20... | collective-permute-start | bytes 786440 | tf_op jit(solution)/shard_map/ppermute | solution.py:21
  (26 other events, 56.7 us)
where the time goes:
time: 143 us; the launch traced here: 142 us
  starting transfers between devices  45.4 us (32%)
  blocking collectives  40.8 us (29%)
  local copies, waits for them, and re-layouts  22.1 us (15%)
  matrix products  16.9 us (12%)
  waiting for transfers between devices  9.57 us (7%)
  other arithmetic  4.91 us (3%)
  between operations  2.14 us (1%)
    ppermute x16, starting transfers between devices, shifted(): return lax.ppermute(block, axis, route)  45.4 us
    psum x1, blocking collectives, body(): counts = lax.psum(local_counts, 'seq')  27.8 us
    unnamed x75, local copies, waits for them, and re-layouts  14.2 us
    pmin x1, blocking collectives, body(): firsts = lax.pmin(local_first, 'seq')  9.82 us
    ppermute x16, waiting for transfers between devices, shifted(): return lax.ppermute(block, axis, route)  9.57 us
    dot_general x5, matrix products, key_terms_of(): jnp.einsum('hqk,qhd->khd', prob.astype(jnp.bfloat16), by_head(g_rows), pr...  4.73 us
    ppermute x4, local copies, waits for them, and re-layouts, shifted(): return lax.ppermute(block, axis, route)  4.59 us
    dot_general x5, matrix products, tile_mix(): jnp.einsum('hqk,khd->qhd', prob.astype(jnp.bfloat16), by_head(v_rows), pr...  3.87 us
  transfers between devices with their start and end apart: 16, of which 8 were waited for; matrix products, arithmetic and copies ran while one was open for 13% of the time, Pallas kernels for 0%

commit v1 on v0

v1 whole, which is shorter than its diff:
```python
import functools
import math

import jax
import jax.numpy as jnp
from jax import lax
from jax.experimental import pallas as pl
from jax.experimental.pallas import tpu as pltpu
from jax.sharding import PartitionSpec as P


HEAD_DIM = 128
WINDOW = 512
MASKED = -1e30
META_ROWS = 16


bf16, f32 = jnp.bfloat16, jnp.float32
VMEM = pl.BlockSpec(memory_space=pltpu.VMEM)


def dot_nt(a, b):
    return lax.dot_general(a, b, (((1,), (1,)), ((), ())), preferred_element_type=f32)


def dot_nn(a, b):
    return lax.dot_general(a, b, (((1,), (0,)), ((), ())), preferred_element_type=f32)


def route_x(n, cross):
    return [(i, i ^ (3 if cross else 2)) for i in range(n)]


def route_diag(n, cross):
    route = []
    for i in range(n):
        j = i + 2 if (i >> 1) & 1 else i - 2
        route.append((i, j ^ cross if 0 <= j < n else i ^ 1))
    return route


def route_even(n, cross):
    return [(i, i ^ (5 if cross else 4)) for i in range(n)]


def route_odd(n, cross):
    route = []
    for i in range(n):
        j = i + 4 if (i >> 2) & 1 else i - 4
        route.append((i, j ^ cross if 0 <= j < n else i ^ 1))
    return route


def place():
    index = lax.axis_index("seq")
    core = lax.rem(index, 2)
    pair = lax.rem(lax.div(index, 2), 2)
    plane_odd = lax.rem(lax.div(index, 4), 2)
    return index, core, pair, plane_odd


def prep_kernel(heads, q, k, v, g, mark, x1, x2, a1, a2, b1, b2, d1, d2, cc):
    _, core, pair, plane_odd = place()
    rows = q.shape[0]
    mark_v = mark[...]
    high = jnp.floor(mark_v * (1.0 / 256.0))
    low = mark_v - high * 256.0
    row = lax.broadcasted_iota(jnp.int32, (META_ROWS, rows), 0)
    meta = jnp.where(row == 0, high, jnp.where(row == 1, low, 0.0)).astype(bf16)
    for ref in (x1, x2, a1, a2, b1, b2, d1, d2):
        ref[2 * heads * rows :, :] = meta
    cc[4 * heads * rows :, :] = meta

    def tile(ref, group, h):
        start = pl.multiple_of((group * heads + h) * HEAD_DIM, HEAD_DIM)
        return ref[:, pl.ds(start, HEAD_DIM)]

    def fill(first, second, group, refs):
        for h in range(heads):
            one, two = tile(first, group, h), tile(second, group, h)
            for ref in refs:
                ref[h * rows : (h + 1) * rows, :] = one
                ref[(heads + h) * rows : (heads + h + 1) * rows, :] = two

    for group, xs, ds, as_, bs in ((core, x1, d1, a1, b1), (1 - core, x2, d2, a2, b2)):

        @pl.when((pair == 0) & (plane_odd == 0))
        def _():
            fill(k, v, group, (xs, as_))
            fill(q, g, group, (ds, bs))

        @pl.when((pair == 0) & (plane_odd == 1))
        def _():
            fill(k, v, group, (xs, bs))
            fill(q, g, group, (ds, as_))

        @pl.when((pair == 1) & (plane_odd == 0))
        def _():
            fill(k, v, group, (ds, as_))
            fill(q, g, group, (xs, bs))

        @pl.when((pair == 1) & (plane_odd == 1))
        def _():
            fill(k, v, group, (ds, bs))
            fill(q, g, group, (xs, as_))

    for n, ref in enumerate((q, g, k, v)):
        for h in range(heads):
            at = (n * heads + h) * rows
            cc[at : at + rows, :] = tile(ref, 1 - core, h)


def marks_of(meta):
    value = meta[0:1, :] * 256.0 + meta[1:2, :]
    doc = jnp.floor(value * 0.5)
    return doc, value - 2.0 * doc


def read_marks(ref, at):
    return marks_of(ref[at : at + META_ROWS, :].astype(f32))


def column_of(row):
    return jnp.transpose(jnp.broadcast_to(row, (HEAD_DIM, row.shape[1])))


def own_marks(mark, cc, heads, rows):
    value = mark[...]
    doc = jnp.floor(value * 0.5)
    other_doc, other_loss = read_marks(cc, 4 * heads * rows)
    return [(doc, value - 2.0 * doc), (other_doc, other_loss)]


def chip_positions(core, rows, axis, shape):
    spot = lax.broadcasted_iota(jnp.int32, shape, axis)
    return spot + jnp.where(spot < rows, core * rows, -core * rows)


def query_kernel(
    heads, chips, q, k, v, g, mark, cc, x1, x2, a1, a2, b1, b2, d1, d2,
    att_own, dq_own, send, stats, bias,
):
    index, core, pair, plane_odd = place()
    chip = lax.div(index, 2)
    rows = q.shape[0]
    scale = 1.0 / math.sqrt(HEAD_DIM)
    is_one, is_odd = pair == 1, plane_odd == 1
    meta_at = 2 * heads * rows

    def either(flag, one, two):
        return jnp.where(flag, one, two)

    def marks(flag, one, two, valid):
        doc_a, loss_a = read_marks(one, meta_at)
        doc_b, loss_b = read_marks(two, meta_at)
        doc = either(flag, doc_a, doc_b)
        return jnp.where(valid, doc, -1.0), either(flag, loss_a, loss_b)

    own = own_marks(mark, cc, heads, rows)
    left_1, left_2 = chip >= 1, chip >= 2
    right_1, right_2 = chip < chips - 1, chip < chips - 2
    m1 = [marks(is_one, x1, d1, left_1), marks(is_one, x2, d2, left_1)]
    m2 = [marks(is_odd, a1, b1, left_2), marks(is_odd, a2, b2, left_2)]
    p1 = [marks(is_one, d1, x1, right_1), marks(is_one, d2, x2, right_1)]
    p2 = [marks(is_odd, b1, a1, right_2), marks(is_odd, b2, a2, right_2)]

    q_doc = column_of(jnp.concatenate([own[0][0], own[1][0]], axis=1))
    q_loss = column_of(jnp.concatenate([own[0][1], own[1][1]], axis=1))
    total = jnp.zeros((2 * rows, HEAD_DIM), f32)
    for doc, loss in own + m1 + m2 + p1 + p2:
        total = total + jnp.where(q_doc == doc, loss, 0.0)
    count = jnp.sum(total, axis=1, keepdims=True)
    weight = q_loss[:, 0:1] * (float(rows) / jnp.maximum(count, float(rows // 8)))

    q_pos = chip_positions(core, rows, 0, (2 * rows, HEAD_DIM))
    spot = lax.broadcasted_iota(jnp.int32, (2 * rows, HEAD_DIM), 1)
    offsets = [core * rows, (1 - core) * rows]
    offsets = offsets + [o - 2 * rows for o in offsets] + [o - 4 * rows for o in offsets]
    for n, (doc, _) in enumerate(own + m1 + m2):
        gap = q_pos - (spot + offsets[n])
        fine = (gap >= 0) & (gap < WINDOW) & (q_doc == doc)
        bias[:, n * rows : (n + 1) * rows] = jnp.where(fine, 0.0, MASKED)

    lane = lax.broadcasted_iota(jnp.int32, (2 * rows, HEAD_DIM), 1)
    table = jnp.where(lane == 2 * heads, weight, 0.0)

    def local(ref, n, h):
        start = pl.multiple_of((core * heads + h) * HEAD_DIM, HEAD_DIM)
        at = (n * heads + h) * rows
        return [ref[:, pl.ds(start, HEAD_DIM)], cc[at : at + rows, :]]

    def halo(n, h):
        at = pl.ds((n * heads + h) * rows, rows)
        return [
            either(is_one, x1[at, :], d1[at, :]),
            either(is_one, x2[at, :], d2[at, :]),
            either(is_odd, a1[at, :], b1[at, :]),
            either(is_odd, a2[at, :], b2[at, :]),
        ]

    for h in range(heads):
        q_rows = jnp.concatenate(local(q, 0, h), axis=0)
        g_rows = jnp.concatenate(local(g, 1, h), axis=0)
        k_rows = jnp.concatenate(local(k, 2, h) + halo(0, h), axis=0)
        v_rows = jnp.concatenate(local(v, 3, h) + halo(1, h), axis=0)
        score = dot_nt(q_rows, k_rows) * scale + bias[...]
        top = jnp.max(score, axis=1, keepdims=True)
        prob = jnp.exp(score - top)
        norm = jnp.sum(prob, axis=1, keepdims=True)
        share = 1.0 / norm
        att = (dot_nn(prob.astype(bf16), v_rows) * share).astype(bf16)
        delta = jnp.sum(g_rows.astype(f32) * att.astype(f32), axis=1, keepdims=True)
        slope = (prob * (dot_nt(g_rows, v_rows) - delta)).astype(bf16)
        dq = (dot_nn(slope, k_rows) * (share * weight * scale)).astype(bf16)
        att_own[:, h * HEAD_DIM : (h + 1) * HEAD_DIM] = att[:rows]
        dq_own[:, h * HEAD_DIM : (h + 1) * HEAD_DIM] = dq[:rows]
        send[h * rows : (h + 1) * rows, :] = att[rows:]
        send[(heads + h) * rows : (heads + h + 1) * rows, :] = dq[rows:]
        table = jnp.where(lane == h, top + jnp.log(norm), table)
        table = jnp.where(lane == heads + h, delta, table)
    stats[...] = jnp.transpose(table)[:META_ROWS, :]


def key_kernel(
    heads, chips, q, k, v, g, mark, cc, x1, x2, a1, a2, b1, b2, d1, d2, stats, stats_1, stats_2,
    dk_own, dv_own, send, bias,
):
    index, core, pair, plane_odd = place()
    chip = lax.div(index, 2)
    rows = q.shape[0]
    scale = 1.0 / math.sqrt(HEAD_DIM)
    is_one, is_odd = pair == 1, plane_odd == 1
    meta_at = 2 * heads * rows

    def either(flag, one, two):
        return jnp.where(flag, one, two)

    def doc_row(flag, one, two, valid):
        doc = either(flag, read_marks(one, meta_at)[0], read_marks(two, meta_at)[0])
        return jnp.where(valid, doc, -1.0)

    own = [m[0] for m in own_marks(mark, cc, heads, rows)]
    right_1, right_2 = chip < chips - 1, chip < chips - 2
    p1 = [doc_row(is_one, d1, x1, right_1), doc_row(is_one, d2, x2, right_1)]
    p2 = [doc_row(is_odd, b1, a1, right_2), doc_row(is_odd, b2, a2, right_2)]
    k_doc = column_of(jnp.concatenate(own, axis=1))
    k_pos = chip_positions(core, rows, 0, (2 * rows, HEAD_DIM))
    spot = lax.broadcasted_iota(jnp.int32, (2 * rows, HEAD_DIM), 1)
    offsets = [core * rows, (1 - core) * rows]
    offsets = offsets + [o + 2 * rows for o in offsets] + [o + 4 * rows for o in offsets]
    for n, doc in enumerate(own + p1 + p2):
        gap = spot + offsets[n] - k_pos
        fine = (gap >= 0) & (gap < WINDOW) & (k_doc == doc)
        bias[:, n * rows : (n + 1) * rows] = jnp.where(fine, 0.0, MASKED)

    def local(ref, n, h):
        start = pl.multiple_of((core * heads + h) * HEAD_DIM, HEAD_DIM)
        at = (n * heads + h) * rows
        return [ref[:, pl.ds(start, HEAD_DIM)], cc[at : at + rows, :]]

    def halo(n, h):
        at = pl.ds((n * heads + h) * rows, rows)
        return [
            either(is_one, d1[at, :], x1[at, :]),
            either(is_one, d2[at, :], x2[at, :]),
            either(is_odd, b1[at, :], a1[at, :]),
            either(is_odd, b2[at, :], a2[at, :]),
        ]

    def line(n):
        return jnp.concatenate([s[n : n + 1, :] for s in (stats, stats_1, stats_2)], axis=1)

    weight = line(2 * heads)
    for h in range(heads):
        k_rows = jnp.concatenate(local(k, 2, h), axis=0)
        v_rows = jnp.concatenate(local(v, 3, h), axis=0)
        q_rows = jnp.concatenate(local(q, 0, h) + halo(0, h), axis=0)
        g_rows = jnp.concatenate(local(g, 1, h) + halo(1, h), axis=0)
        score = dot_nt(k_rows, q_rows) * scale + bias[...]
        prob = jnp.exp(score - line(h)) * weight
        slope = (prob * (dot_nt(v_rows, g_rows) - line(heads + h))).astype(bf16)
        dv = dot_nn(prob.astype(bf16), g_rows).astype(bf16)
        dk = (dot_nn(slope, q_rows) * scale).astype(bf16)
        dk_own[:, h * HEAD_DIM : (h + 1) * HEAD_DIM] = dk[:rows]
        dv_own[:, h * HEAD_DIM : (h + 1) * HEAD_DIM] = dv[:rows]
        send[h * rows : (h + 1) * rows, :] = dk[rows:]
        send[(heads + h) * rows : (heads + h + 1) * rows, :] = dv[rows:]


def join_kernel(heads, one, two, got, out_one, out_two):
    _, core, _, _ = place()
    rows, half = one.shape
    here = pl.multiple_of(core * half, HEAD_DIM)
    out_one[:, pl.ds(here, half)] = one[...]
    out_two[:, pl.ds(here, half)] = two[...]
    for n, out in enumerate((out_one, out_two)):
        for h in range(heads):
            at = (n * heads + h) * rows
            start = pl.multiple_of((1 - core) * half + h * HEAD_DIM, HEAD_DIM)
            out[:, pl.ds(start, HEAD_DIM)] = got[at : at + rows, :]


def run(kernel, outs, args, scratch=(), flops=0):
    size = sum(math.prod(a.shape) * a.dtype.itemsize for a in args)
    size = size + sum(math.prod(o.shape) * o.dtype.itemsize for o in outs)
    return pl.pallas_call(
        kernel,
        out_shape=outs,
        in_specs=[VMEM] * len(args),
        out_specs=[VMEM] * len(outs),
        scratch_shapes=list(scratch),
        cost_estimate=pl.CostEstimate(flops=flops, bytes_accessed=size, transcendentals=0),
    )(*args)


def body(queries, keys, values, grad_out, doc_ids, loss_mask):
    rows, width = queries.shape
    heads = width // HEAD_DIM // 2
    half = heads * HEAD_DIM
    n = lax.axis_size("seq")
    chips = n // 2
    shape = jax.ShapeDtypeStruct

    def move(value, route, axis="seq"):
        return lax.ppermute(value, axis, route)

    mine = (doc_ids * 2 + loss_mask).astype(f32)
    theirs = move(mine, [(0, 1), (1, 0)], "head")
    first = lax.axis_index("head") == 0
    mark = jnp.concatenate([jnp.where(first, mine, theirs), jnp.where(first, theirs, mine)])
    mark = mark[None, :]

    bundle = shape((2 * heads * rows + META_ROWS, HEAD_DIM), bf16)
    double = shape((4 * heads * rows + META_ROWS, HEAD_DIM), bf16)
    packs = run(
        functools.partial(prep_kernel, heads),
        [bundle] * 8 + [double],
        (queries, keys, values, grad_out, mark),
    )
    x1, x2, a1, a2, b1, b2, d1, d2, cc = packs
    x1 = move(x1, route_x(n, 0))
    a1 = move(a1, route_even(n, 0))
    b1 = move(b1, route_odd(n, 0))
    d1 = move(d1, route_diag(n, 0))
    x2 = move(x2, route_x(n, 1))
    a2 = move(a2, route_even(n, 1))
    b2 = move(b2, route_odd(n, 1))
    d2 = move(d2, route_diag(n, 1))
    cc = move(cc, [(i, i ^ 1) for i in range(n)])

    common = (queries, keys, values, grad_out, mark, cc, x1, x2, a1, a2, b1, b2, d1, d2)
    side = shape((rows, half), bf16)
    pack = shape((2 * heads * rows, HEAD_DIM), bf16)
    table = shape((META_ROWS, 2 * rows), f32)
    bias = pltpu.VMEM((2 * rows, 6 * rows), f32)
    flops = 4 * heads * 2 * (2 * rows) * (6 * rows) * HEAD_DIM
    att, dq, send_1, stats = run(
        functools.partial(query_kernel, heads, chips),
        [side, side, pack, table],
        common,
        [bias],
        flops,
    )
    stats_1 = move(stats, [(i, (i - 2) % n) for i in range(n)])
    stats_2 = move(stats, [(i, (i - 4) % n) for i in range(n)])
    got_1 = move(send_1, [(i, i ^ 1) for i in range(n)])
    dk, dv, send_2 = run(
        functools.partial(key_kernel, heads, chips),
        [side, side, pack],
        common + (stats, stats_1, stats_2),
        [bias],
        flops,
    )
    got_2 = move(send_2, [(i, i ^ 1) for i in range(n)])
    whole = shape((rows, width), bf16)
    join = functools.partial(join_kernel, heads)
    attended, query_grad = run(join, [whole, whole], (att, dq, got_1))
    key_grad, value_grad = run(join, [whole, whole], (dk, dv, got_2))
    return attended, query_grad, key_grad, value_grad


def solution(mesh):
    wide = P("seq", "head")
    flat = P(("seq", "head"))
    return jax.shard_map(
        body,
        mesh=mesh,
        in_specs=(wide, wide, wide, wide, flat, flat),
        out_specs=(wide, wide, wide, wide),
        check_vma=False,
    )
```

time: 143 us -> 66.2 us (0.46)
  the two profiles are of different devices: /device:TPU:7 before, /device:TPU:23 now
where the time goes in v1:
time: 66.2 us; the launch traced here: 66 us
  waiting for transfers between devices  24.8 us (37%)
  Pallas kernels  18.2 us (27%)
  starting transfers between devices  17.4 us (26%)
  local copies, waits for them, and re-layouts  3.49 us (5%)
  other arithmetic  1.27 us (2%)
  between operations  0.72 us (1%)
    ppermute x14, waiting for transfers between devices, move(): return lax.ppermute(value, axis, route)  24.8 us
    pallas_call x5, Pallas kernels, run(): pl.pallas_call(kernel, out_shape=outs, in_specs=[VMEM] * len(args), out_s...  18.2 us
    ppermute x14, starting transfers between devices, move(): return lax.ppermute(value, axis, route)  17.4 us
    unnamed x26, local copies, waits for them, and re-layouts  3.49 us
  transfers between devices with their start and end apart: 14, of which 7 were waited for; matrix products, arithmetic and copies ran while one was open for 0% of the time, Pallas kernels for 10%

profile of v1, /device:TPU:23, one launch (start us, length us, event | category | flops | bytes accessed | tf_op | source)
XLA Modules:
  0.0 66.0 jit_solution(13386093751260015503)
XLA Ops:
  0.6 0.7 %add_convert_fusion = f32[64]{0:T(128)S(1)} fusion(s32[64]{0:T(128)} %param.11, s32[64]{0:T(128)} %param.10), kind=kLoop, calls=%fused_computation.3 | loop fusion | flops 192 | bytes 768 | tf_op jit(solution)/shard_map/convert_element_type | solution.py:327
  1.5 2.2 %collective-permute-done = f32[64]{0:T(128)S(1)} collective-permute-done((f32[64]{0:T(128)S(1)}, f32[64]{0:T(128)S(1)}, u32[]{:S(2)}, u32[]{:S(2)}) %collective-permute-start) | collective-permute-done | bytes 288 | tf_op jit(solution)/shard_map/ppermute | solution.py:325
  4.3 3.2 %shard_map.93 = (bf16[1040,128]{1,0:T(8,128)(2,1)}, bf16[1040,128]{1,0:T(8,128)(2,1)}, bf16[1040,128]{1,0:T(8,128)(2,1)}, bf16[1040,128]{1,0:T(8,128)(2,1)}, bf1...) custom-call(bf16[128,1024]{1,0:T(8,128)(2,1)} %q.5, ...), custom_call_target="tpu_custom_call" | custom-call | bytes 3707392 | tf_op jit(solution)/shard_map/pallas_call | solution.py:306
  7.7 3.2 %collective-permute-start.3 = (bf16[1040,128]{1,0:T(8,128)(2,1)}, bf16[1040,128]{1,0:T(8,128)(2,1)S(1)}, u32[]{:S(2)}, u32[]{:S(2)}) collective-permute-start(bf16[1040,128]{1,0:T(8,128)(2,1)} %get-tuple-element.26), channel_id=1, source_target_pairs={{0,6},{2,4},{4,2},{6,0},{8,14},{10,12},{12,10},{14,8},{16,22},{18,... | collective-permute-start | bytes 798728 | tf_op jit(solution)/shard_map/ppermute | solution.py:325
  10.9 1.3 %collective-permute-start.4 = (bf16[1040,128]{1,0:T(8,128)(2,1)}, bf16[1040,128]{1,0:T(8,128)(2,1)S(1)}, u32[]{:S(2)}, u32[]{:S(2)}) collective-permute-start(bf16[1040,128]{1,0:T(8,128)(2,1)} %get-tuple-element.27), channel_id=1, source_target_pairs={{0,8},{2,10},{4,12},{6,14},{8,0},{10,2},{12,4},{14,6},{16,24},{18,... | collective-permute-start | bytes 798728 | tf_op jit(solution)/shard_map/ppermute | solution.py:325
  12.8 1.0 %collective-permute-done.2.x1 = bf16[1040,128]{1,0:T(8,128)(2,1)S(1)} collective-permute-done((bf16[1040,128]{1,0:T(8,128)(2,1)}, bf16[1040,128]{1,0:T(8,128)(2,1)S(1)}, u32[]{:S(2)}, u32[]{:S(2)}) %collective-permute-start.2) | collective-permute-done | bytes 266272 | tf_op jit(solution)/shard_map/ppermute | solution.py:325
  14.0 7.8 %collective-permute-done.3.x2 = bf16[1040,128]{1,0:T(8,128)(2,1)S(1)} collective-permute-done((bf16[1040,128]{1,0:T(8,128)(2,1)}, bf16[1040,128]{1,0:T(8,128)(2,1)S(1)}, u32[]{:S(2)}, u32[]{:S(2)}) %collective-permute-start.3) | collective-permute-done | bytes 266272 | tf_op jit(solution)/shard_map/ppermute | solution.py:325
  21.8 1.3 %collective-permute-start.8 = (bf16[1040,128]{1,0:T(8,128)(2,1)}, bf16[1040,128]{1,0:T(8,128)(2,1)S(1)}, u32[]{:S(2)}, u32[]{:S(2)}) collective-permute-start(bf16[1040,128]{1,0:T(8,128)(2,1)} %get-tuple-element.31), channel_id=1, source_target_pairs={{0,2},{2,0},{4,8},{6,10},{8,4},{10,6},{12,16},{14,18},{16,12},{18,... | collective-permute-start | bytes 798728 | tf_op jit(solution)/shard_map/ppermute | solution.py:325
  23.2 0.8 %collective-permute-done.5.a2 = bf16[1040,128]{1,0:T(8,128)(2,1)S(1)} collective-permute-done((bf16[1040,128]{1,0:T(8,128)(2,1)}, bf16[1040,128]{1,0:T(8,128)(2,1)S(1)}, u32[]{:S(2)}, u32[]{:S(2)}) %collective-permute-start.5) | collective-permute-done | bytes 266272 | tf_op jit(solution)/shard_map/ppermute | solution.py:325
  24.0 2.5 %collective-permute-start.9 = (bf16[1040,128]{1,0:T(8,128)(2,1)}, bf16[1040,128]{1,0:T(8,128)(2,1)S(1)}, u32[]{:S(2)}, u32[]{:S(2)}) collective-permute-start(bf16[1040,128]{1,0:T(8,128)(2,1)} %get-tuple-element.32), channel_id=1, source_target_pairs={{0,2},{2,0},{4,10},{6,8},{8,6},{10,4},{12,18},{14,16},{16,14},{18,... | collective-permute-start | bytes 798728 | tf_op jit(solution)/shard_map/ppermute | solution.py:325
  26.5 5.8 %collective-permute-done.7.b2 = bf16[1040,128]{1,0:T(8,128)(2,1)S(1)} collective-permute-done((bf16[1040,128]{1,0:T(8,128)(2,1)}, bf16[1040,128]{1,0:T(8,128)(2,1)S(1)}, u32[]{:S(2)}, u32[]{:S(2)}) %collective-permute-start.7) | collective-permute-done | bytes 266272 | tf_op jit(solution)/shard_map/ppermute | solution.py:325
  32.3 4.5 %collective-permute-done.9.d2 = bf16[1040,128]{1,0:T(8,128)(2,1)S(1)} collective-permute-done((bf16[1040,128]{1,0:T(8,128)(2,1)}, bf16[1040,128]{1,0:T(8,128)(2,1)S(1)}, u32[]{:S(2)}, u32[]{:S(2)}) %collective-permute-start.9) | collective-permute-done | bytes 266272 | tf_op jit(solution)/shard_map/ppermute | solution.py:325
  36.9 0.6 copy-done.8
  37.5 0.8 %copy-done = bf16[2064,128]{1,0:T(8,128)(2,1)} copy-done((bf16[2064,128]{1,0:T(8,128)(2,1)}, bf16[2064,128]{1,0:T(8,128)(2,1)S(1)}, u32[]{:S(2)}) %copy-start) | copy-done | bytes 528408
  38.4 6.2 %shard_map.94 = (bf16[128,512]{1,0:T(8,128)(2,1)}, bf16[128,512]{1,0:T(8,128)(2,1)}, bf16[1024,128]{1,0:T(8,128)(2,1)}, f32[16,256]{1,0:T(8,128)}) custom-call(bf16[128,1024]{1,0:T(8,128)(2,1)} %q.5, bf16[128,1024]{1,0:T(8,128)(2,1)} %k.5, bf16[128,1024]{1,0:T(8,128)(2,1)} %v.5, bf16[128,1024]{1,0:T(8,128)(2,1)} %g.5, f32[1,128]{1,0:T(1,128)} %maximum_bitcast_fusion.mark, ...), custom_call_target="tpu_custom_call" | custom-call | flops 805306368 | bytes 4248064 | tf_op jit(solution)/shard_map/pallas_call | solution.py:306
  44.6 5.2 %collective-permute-start.12 = (f32[16,256]{1,0:T(8,128)}, f32[16,256]{1,0:T(8,128)S(1)}, u32[]{:S(2)}, u32[]{:S(2)}) collective-permute-start(f32[16,256]{1,0:T(8,128)} %get-tuple-element.38.stats), channel_id=1, source_target_pairs={{0,24},{2,26},{4,28},{6,30},{8,0},{10,2},{12,4},{14,6},{16,8},{18,... | collective-permute-start | bytes 49160 | tf_op jit(solution)/shard_map/ppermute | solution.py:325
  49.7 1.1 %collective-permute-start.11 = (f32[16,256]{1,0:T(8,128)}, f32[16,256]{1,0:T(8,128)S(1)}, u32[]{:S(2)}, u32[]{:S(2)}) collective-permute-start(f32[16,256]{1,0:T(8,128)} %get-tuple-element.38.stats), channel_id=1, source_target_pairs={{0,28},{2,30},{4,0},{6,2},{8,4},{10,6},{12,8},{14,10},{16,12},{18,... | collective-permute-start | bytes 49160 | tf_op jit(solution)/shard_map/ppermute | solution.py:325
  50.8 2.6 %collective-permute-done.11.stats_1 = f32[16,256]{1,0:T(8,128)S(1)} collective-permute-done((f32[16,256]{1,0:T(8,128)}, f32[16,256]{1,0:T(8,128)S(1)}, u32[]{:S(2)}, u32[]{:S(2)}) %collective-permute-start.11) | collective-permute-done | bytes 16416 | tf_op jit(solution)/shard_map/ppermute | solution.py:325
  54.1 5.0 %shard_map.96 = (bf16[128,512]{1,0:T(8,128)(2,1)}, bf16[128,512]{1,0:T(8,128)(2,1)}, bf16[1024,128]{1,0:T(8,128)(2,1)}) custom-call(bf16[128,1024]{1,0:T(8,128)(2,1)} %q.5, bf16[128,1024]{1,0:T(8,128)(2,1)} %k.5, bf16[128,1024]{1,0:T(8,128)(2,1)} %v.5, bf16[128,1024]{1,0:T(8,128)(2,1)} %g.5, f32[1,128]{1,0:T(1,128)} %maximum_bitcast_fusion.mark, ...), custom_call_target="tpu_custom_call" | custom-call | flops 805306368 | bytes 4280832 | tf_op jit(solution)/shard_map/pallas_call | solution.py:306
  59.1 1.6 %collective-permute-start.13 = (bf16[1024,128]{1,0:T(8,128)(2,1)}, bf16[1024,128]{1,0:T(8,128)(2,1)S(1)}, u32[]{:S(2)}, u32[]{:S(2)}) collective-permute-start(bf16[1024,128]{1,0:T(8,128)(2,1)} %get-tuple-element.41), channel_id=1, source_target_pairs={{0,2},{2,0},{4,6},{6,4},{8,10},{10,8},{12,14},{14,12},{16,18},{18,... | collective-permute-start | bytes 786440 | tf_op jit(solution)/shard_map/ppermute | solution.py:325
  60.7 0.7 %copy-done.9 = bf16[1024,128]{1,0:T(8,128)(2,1)} copy-done((bf16[1024,128]{1,0:T(8,128)(2,1)}, bf16[1024,128]{1,0:T(8,128)(2,1)S(1)}, u32[]{:S(2)}) %copy-start.9) | copy-done | bytes 262168
  61.4 1.9 %shard_map.95 = (bf16[128,1024]{1,0:T(8,128)(2,1)}, bf16[128,1024]{1,0:T(8,128)(2,1)}) custom-call(bf16[128,512]{1,0:T(8,128)(2,1)} %get-tuple-element.33.one, bf16[128,512]{1,0:T(8,128)(2,1)} %get-tuple-element.34.two, bf16[1024,128]{1,0:T(8,128)(2,1)} %copy-done.9), custom_call_target="tpu_custom_call" | custom-call | bytes 1048576 | tf_op jit(solution)/shard_map/pallas_call | solution.py:306
  63.3 0.7 %copy-done.10 = bf16[1024,128]{1,0:T(8,128)(2,1)} copy-done((bf16[1024,128]{1,0:T(8,128)(2,1)}, bf16[1024,128]{1,0:T(8,128)(2,1)S(1)}, u32[]{:S(2)}) %copy-start.10) | copy-done | bytes 262168
  64.0 1.9 %shard_map.97 = (bf16[128,1024]{1,0:T(8,128)(2,1)}, bf16[128,1024]{1,0:T(8,128)(2,1)}) custom-call(bf16[128,512]{1,0:T(8,128)(2,1)} %get-tuple-element.39.one, bf16[128,512]{1,0:T(8,128)(2,1)} %get-tuple-element.40.two, bf16[1024,128]{1,0:T(8,128)(2,1)} %copy-done.10), custom_call_target="tpu_custom_call" | custom-call | bytes 1048576 | tf_op jit(solution)/shard_map/pallas_call | solution.py:306
  (38 shorter events, 2.5 us)
Async XLA Ops:
  1.3 2.4 %collective-permute-start = (f32[64]{0:T(128)S(1)}, f32[64]{0:T(128)S(1)}, u32[]{:S(2)}, u32[]{:S(2)}) collective-permute-start(f32[64]{0:T(128)S(1)} %add_convert_fusion), channel_id=1, source_target_pairs={{0,1},{1,0},{2,3},{3,2},{4,5},{5,4},{6,7},{7,6},{8,9},{9,8},{10,11... | collective-permute-start | bytes 776 | tf_op jit(solution)/shard_map/ppermute | solution.py:325
  7.5 6.3 %collective-permute-start.2 = (bf16[1040,128]{1,0:T(8,128)(2,1)}, bf16[1040,128]{1,0:T(8,128)(2,1)S(1)}, u32[]{:S(2)}, u32[]{:S(2)}) collective-permute-start(bf16[1040,128]{1,0:T(8,128)(2,1)} %get-tuple-element.25), channel_id=1, source_target_pairs={{0,4},{2,6},{4,0},{6,2},{8,12},{10,14},{12,8},{14,10},{16,20},{18,... | collective-permute-start | bytes 798728 | tf_op jit(solution)/shard_map/ppermute | solution.py:325
  7.7 14.1 %collective-permute-start.3 = (bf16[1040,128]{1,0:T(8,128)(2,1)}, bf16[1040,128]{1,0:T(8,128)(2,1)S(1)}, u32[]{:S(2)}, u32[]{:S(2)}) collective-permute-start(bf16[1040,128]{1,0:T(8,128)(2,1)} %get-tuple-element.26), channel_id=1, source_target_pairs={{0,6},{2,4},{4,2},{6,0},{8,14},{10,12},{12,10},{14,8},{16,22},{18,... | collective-permute-start | bytes 798728 | tf_op jit(solution)/shard_map/ppermute | solution.py:325
  10.9 10.9 %collective-permute-start.4 = (bf16[1040,128]{1,0:T(8,128)(2,1)}, bf16[1040,128]{1,0:T(8,128)(2,1)S(1)}, u32[]{:S(2)}, u32[]{:S(2)}) collective-permute-start(bf16[1040,128]{1,0:T(8,128)(2,1)} %get-tuple-element.27), channel_id=1, source_target_pairs={{0,8},{2,10},{4,12},{6,14},{8,0},{10,2},{12,4},{14,6},{16,24},{18,... | collective-permute-start | bytes 798728 | tf_op jit(solution)/shard_map/ppermute | solution.py:325
  12.2 11.8 %collective-permute-start.5 = (bf16[1040,128]{1,0:T(8,128)(2,1)}, bf16[1040,128]{1,0:T(8,128)(2,1)S(1)}, u32[]{:S(2)}, u32[]{:S(2)}) collective-permute-start(bf16[1040,128]{1,0:T(8,128)(2,1)} %get-tuple-element.28), channel_id=1, source_target_pairs={{0,10},{2,8},{4,14},{6,12},{8,2},{10,0},{12,6},{14,4},{16,26},{18,... | collective-permute-start | bytes 798728 | tf_op jit(solution)/shard_map/ppermute | solution.py:325
  12.2 24.6 %collective-permute-start.1 = (bf16[2064,128]{1,0:T(8,128)(2,1)}, bf16[2064,128]{1,0:T(8,128)(2,1)S(1)}, u32[]{:S(2)}, u32[]{:S(2)}) collective-permute-start(bf16[2064,128]{1,0:T(8,128)(2,1)} %get-tuple-element.24), channel_id=1, source_target_pairs={{0,2},{2,0},{4,6},{6,4},{8,10},{10,8},{12,14},{14,12},{16,18},{18,... | collective-permute-start | bytes 1585160 | tf_op jit(solution)/shard_map/ppermute | solution.py:325
  13.8 23.0 %copy-start.1 = (bf16[1040,128]{1,0:T(8,128)(2,1)}, bf16[1040,128]{1,0:T(8,128)(2,1)S(1)}, u32[]{:S(2)}) copy-start(bf16[1040,128]{1,0:T(8,128)(2,1)S(1)} %collective-permute-done.2.x1) | copy-start | bytes 798724
  13.8 12.7 %collective-permute-start.6 = (bf16[1040,128]{1,0:T(8,128)(2,1)}, bf16[1040,128]{1,0:T(8,128)(2,1)S(1)}, u32[]{:S(2)}, u32[]{:S(2)}) collective-permute-start(bf16[1040,128]{1,0:T(8,128)(2,1)} %get-tuple-element.29), channel_id=1, source_target_pairs={{0,2},{2,0},{4,6},{6,4},{8,16},{10,18},{12,20},{14,22},{16,8},{18,... | collective-permute-start | bytes 798728 | tf_op jit(solution)/shard_map/ppermute | solution.py:325
  21.8 15.0 %copy-start.2 = (bf16[1040,128]{1,0:T(8,128)(2,1)}, bf16[1040,128]{1,0:T(8,128)(2,1)S(1)}, u32[]{:S(2)}) copy-start(bf16[1040,128]{1,0:T(8,128)(2,1)S(1)} %collective-permute-done.3.x2) | copy-start | bytes 798724
  21.8 10.5 %collective-permute-start.7 = (bf16[1040,128]{1,0:T(8,128)(2,1)}, bf16[1040,128]{1,0:T(8,128)(2,1)S(1)}, u32[]{:S(2)}, u32[]{:S(2)}) collective-permute-start(bf16[1040,128]{1,0:T(8,128)(2,1)} %get-tuple-element.30), channel_id=1, source_target_pairs={{0,2},{2,0},{4,6},{6,4},{8,18},{10,16},{12,22},{14,20},{16,10},{18... | collective-permute-start | bytes 798728 | tf_op jit(solution)/shard_map/ppermute | solution.py:325
  21.8 15.0 %copy-start.3 = (bf16[1040,128]{1,0:T(8,128)(2,1)}, bf16[1040,128]{1,0:T(8,128)(2,1)S(1)}, u32[]{:S(2)}) copy-start(bf16[1040,128]{1,0:T(8,128)(2,1)S(1)} %collective-permute-done.4.a1) | copy-start | bytes 798724
  21.8 10.5 %collective-permute-start.8 = (bf16[1040,128]{1,0:T(8,128)(2,1)}, bf16[1040,128]{1,0:T(8,128)(2,1)S(1)}, u32[]{:S(2)}, u32[]{:S(2)}) collective-permute-start(bf16[1040,128]{1,0:T(8,128)(2,1)} %get-tuple-element.31), channel_id=1, source_target_pairs={{0,2},{2,0},{4,8},{6,10},{8,4},{10,6},{12,16},{14,18},{16,12},{18,... | collective-permute-start | bytes 798728 | tf_op jit(solution)/shard_map/ppermute | solution.py:325
  24.0 12.8 %copy-start.4 = (bf16[1040,128]{1,0:T(8,128)(2,1)}, bf16[1040,128]{1,0:T(8,128)(2,1)S(1)}, u32[]{:S(2)}) copy-start(bf16[1040,128]{1,0:T(8,128)(2,1)S(1)} %collective-permute-done.5.a2) | copy-start | bytes 798724
  24.0 12.8 %collective-permute-start.9 = (bf16[1040,128]{1,0:T(8,128)(2,1)}, bf16[1040,128]{1,0:T(8,128)(2,1)S(1)}, u32[]{:S(2)}, u32[]{:S(2)}) collective-permute-start(bf16[1040,128]{1,0:T(8,128)(2,1)} %get-tuple-element.32), channel_id=1, source_target_pairs={{0,2},{2,0},{4,10},{6,8},{8,6},{10,4},{12,18},{14,16},{16,14},{18,... | collective-permute-start | bytes 798728 | tf_op jit(solution)/shard_map/ppermute | solution.py:325
  26.5 10.4 %copy-start.5 = (bf16[1040,128]{1,0:T(8,128)(2,1)}, bf16[1040,128]{1,0:T(8,128)(2,1)S(1)}, u32[]{:S(2)}) copy-start(bf16[1040,128]{1,0:T(8,128)(2,1)S(1)} %collective-permute-done.6.b1) | copy-start | bytes 798724
  32.3 4.6 %copy-start.6 = (bf16[1040,128]{1,0:T(8,128)(2,1)}, bf16[1040,128]{1,0:T(8,128)(2,1)S(1)}, u32[]{:S(2)}) copy-start(bf16[1040,128]{1,0:T(8,128)(2,1)S(1)} %collective-permute-done.7.b2) | copy-start | bytes 798724
  32.3 4.6 %copy-start.7 = (bf16[1040,128]{1,0:T(8,128)(2,1)}, bf16[1040,128]{1,0:T(8,128)(2,1)S(1)}, u32[]{:S(2)}) copy-start(bf16[1040,128]{1,0:T(8,128)(2,1)S(1)} %collective-permute-done.8.d1) | copy-start | bytes 798724
  36.8 0.7 %copy-start.8 = (bf16[1040,128]{1,0:T(8,128)(2,1)}, bf16[1040,128]{1,0:T(8,128)(2,1)S(1)}, u32[]{:S(2)}) copy-start(bf16[1040,128]{1,0:T(8,128)(2,1)S(1)} %collective-permute-done.9.d2) | copy-start | bytes 798724
  37.5 0.8 %copy-start = (bf16[2064,128]{1,0:T(8,128)(2,1)}, bf16[2064,128]{1,0:T(8,128)(2,1)S(1)}, u32[]{:S(2)}) copy-start(bf16[2064,128]{1,0:T(8,128)(2,1)S(1)} %collective-permute-done.1.cc) | copy-start | bytes 1585156
  44.6 6.3 %collective-permute-start.12 = (f32[16,256]{1,0:T(8,128)}, f32[16,256]{1,0:T(8,128)S(1)}, u32[]{:S(2)}, u32[]{:S(2)}) collective-permute-start(f32[16,256]{1,0:T(8,128)} %get-tuple-element.38.stats), channel_id=1, source_target_pairs={{0,24},{2,26},{4,28},{6,30},{8,0},{10,2},{12,4},{14,6},{16,8},{18,... | collective-permute-start | bytes 49160 | tf_op jit(solution)/shard_map/ppermute | solution.py:325
  49.7 3.7 %collective-permute-start.11 = (f32[16,256]{1,0:T(8,128)}, f32[16,256]{1,0:T(8,128)S(1)}, u32[]{:S(2)}, u32[]{:S(2)}) collective-permute-start(f32[16,256]{1,0:T(8,128)} %get-tuple-element.38.stats), channel_id=1, source_target_pairs={{0,28},{2,30},{4,0},{6,2},{8,4},{10,6},{12,8},{14,10},{16,12},{18,... | collective-permute-start | bytes 49160 | tf_op jit(solution)/shard_map/ppermute | solution.py:325
  50.8 9.9 %collective-permute-start.10 = (bf16[1024,128]{1,0:T(8,128)(2,1)}, bf16[1024,128]{1,0:T(8,128)(2,1)S(1)}, u32[]{:S(2)}, u32[]{:S(2)}) collective-permute-start(bf16[1024,128]{1,0:T(8,128)(2,1)} %get-tuple-element.35), channel_id=1, source_target_pairs={{0,2},{2,0},{4,6},{6,4},{8,10},{10,8},{12,14},{14,12},{16,18},{18,... | collective-permute-start | bytes 786440 | tf_op jit(solution)/shard_map/ppermute | solution.py:325
  50.8 2.6 %copy-start.11 = (f32[16,256]{1,0:T(8,128)}, f32[16,256]{1,0:T(8,128)S(1)}, u32[]{:S(2)}) copy-start(f32[16,256]{1,0:T(8,128)S(1)} %collective-permute-done.12.stats_2) | copy-start | bytes 49156
  59.1 4.3 %collective-permute-start.13 = (bf16[1024,128]{1,0:T(8,128)(2,1)}, bf16[1024,128]{1,0:T(8,128)(2,1)S(1)}, u32[]{:S(2)}, u32[]{:S(2)}) collective-permute-start(bf16[1024,128]{1,0:T(8,128)(2,1)} %get-tuple-element.41), channel_id=1, source_target_pairs={{0,2},{2,0},{4,6},{6,4},{8,10},{10,8},{12,14},{14,12},{16,18},{18,... | collective-permute-start | bytes 786440 | tf_op jit(solution)/shard_map/ppermute | solution.py:325
  (3 other events, 2.0 us)
